TPU v7x, 256 devices: a whole 4x4x8 slice. The times are simulated.
256 devices in a mesh: dp: 16 (over z, x_lo), tensor: 16 (over y, x_hi, core).
Axes of the slice: x: 4 (x_hi: 2, x_lo: 2; x = x_hi * 2 + x_lo), y: 4, z: 8, core: 2. Of those that a mesh axis runs over, the one named last changes fastest.
Arguments:
- activations: bfloat16 [8192, 32768], P('tensor', 'dp'), may hold values from -6 to 6
- cotangent: bfloat16 [8192, 32768], P('tensor', 'dp'), may hold values from -6 to 6
- first_up: bfloat16 [64, 128, 128], P('tensor', 'dp'), may hold values from -0.5 to 0.5
- second_up: bfloat16 [128, 64, 256], P('tensor', 'dp'), may hold values from -0.75 to 0.75
- second_down: bfloat16 [128, 64, 256], P('tensor', 'dp'), may hold values from -0.375 to 0.375
- first_down: bfloat16 [64, 128, 128], P('tensor', 'dp'), may hold values from -0.5 to 0.5
Outputs:
- output: bfloat16 [8192, 32768], P('tensor', 'dp')
- grad_input: bfloat16 [8192, 32768], P('tensor', 'dp')
- grad_first_up: float32 [64, 128, 128], P('tensor', 'dp')
- grad_second_up: float32 [128, 64, 256], P('tensor', 'dp')
- grad_second_down: float32 [128, 64, 256], P('tensor', 'dp')
- grad_first_down: float32 [64, 128, 128], P('tensor', 'dp')
All inputs are finite; a program needn't handle non-finite values.
Results may differ from a plain program's by a relative error of at most 0.007.
Values may be sent and summed in bfloat16 or wider, within the bound.
A program may use at most 128 MiB of HBM per device.

v0:
```python
import jax
import jax.numpy as jnp
from jax import lax
from jax.sharding import PartitionSpec as P


def gelu_value(v):
    return 0.5 * v * (1.0 + lax.erf(v * 0.7071067811865476))


def gelu_slope(v):
    return (
        0.5 * (1.0 + lax.erf(v * 0.7071067811865476))
        + v * jnp.exp(-0.5 * v * v) * 0.3989422804014327
    )


def product(form, left, right):
    return jnp.einsum(form, left, right, preferred_element_type=jnp.float32)


def transpose_blocks(values):
    return lax.all_to_all(values, "tensor", split_axis=1, concat_axis=0, tiled=True)


def restore_blocks(values):
    return lax.all_to_all(values, "tensor", split_axis=0, concat_axis=1, tiled=True)


def local(activations, cotangent, first_up, second_up, second_down, first_down):
    width_local, tokens = activations.shape
    blocks_local = first_up.shape[0]
    block_size = first_up.shape[2]
    inputs = activations.reshape(blocks_local, block_size, tokens)
    grads_in = cotangent.reshape(blocks_local, block_size, tokens)
    up_one, up_two, down_two, down_one = (
        lax.all_gather(first_up, "dp", axis=1, tiled=True),
        lax.all_gather(second_up, "dp", axis=1, tiled=True),
        lax.all_gather(second_down, "dp", axis=1, tiled=True),
        lax.all_gather(first_down, "dp", axis=1, tiled=True),
    )
    section_one = product("kit,kij->kjt", inputs, up_one).astype(jnp.bfloat16)
    moved_one = transpose_blocks(section_one)
    pre = product("kjt,jkm->jmt", moved_one, up_two)
    hid = gelu_value(pre).astype(jnp.bfloat16)
    section_three = product("jmt,jkm->kjt", hid, down_two).astype(jnp.bfloat16)
    moved_three = restore_blocks(section_three)
    result = product("kjt,kji->kit", moved_three, down_one).astype(jnp.bfloat16)
    part_r2 = product("kjt,kit->kji", moved_three, grads_in)
    back_three = product("kit,kji->kjt", grads_in, down_one).astype(jnp.bfloat16)
    moved_back = transpose_blocks(back_three)
    part_l2 = product("jmt,kjt->jkm", hid, moved_back)
    back_hid = product("kjt,jkm->jmt", moved_back, down_two)
    back_pre = (back_hid * gelu_slope(pre)).astype(jnp.bfloat16)
    part_l1 = product("kjt,jmt->jkm", moved_one, back_pre)
    back_one = product("jmt,jkm->kjt", back_pre, up_two).astype(jnp.bfloat16)
    local_back = restore_blocks(back_one)
    part_r1 = product("kit,kjt->kij", inputs, local_back)
    grad_in = product("kjt,kij->kit", local_back, up_one).astype(jnp.bfloat16)
    sum_r1, sum_l1, sum_l2, sum_r2 = (
        lax.psum_scatter(part_r1, "dp", scatter_dimension=1, tiled=True),
        lax.psum_scatter(part_l1, "dp", scatter_dimension=1, tiled=True),
        lax.psum_scatter(part_l2, "dp", scatter_dimension=1, tiled=True),
        lax.psum_scatter(part_r2, "dp", scatter_dimension=1, tiled=True),
    )
    output = result.reshape(width_local, tokens)
    grad_input = grad_in.reshape(width_local, tokens)
    return (output, grad_input, sum_r1, sum_l1, sum_l2, sum_r2)


def solution(mesh):
    in_specs = (
        P("tensor", "dp"),
        P("tensor", "dp"),
        P("tensor", "dp", None),
        P("tensor", "dp", None),
        P("tensor", "dp", None),
        P("tensor", "dp", None),
    )
    out_specs = (
        P("tensor", "dp"),
        P("tensor", "dp"),
        P("tensor", "dp", None),
        P("tensor", "dp", None),
        P("tensor", "dp", None),
        P("tensor", "dp", None),
    )
    return jax.shard_map(local, mesh=mesh, in_specs=in_specs, out_specs=out_specs, check_vma=False)
```

profile of v0, /device:TPU:1, one launch (start us, length us, event | category | flops | bytes accessed | tf_op | source)
XLA Modules:
  0.0 601.9 jit_solution(7144741162166313327)
XLA Ops:
  7.2 31.1 %all_gather.12 = bf16[4,128,128]{2,1,0:T(8,128)(2,1)S(1)} all-gather(bf16[4,8,128]{2,1,0:T(8,128)(2,1)} %param.8), channel_id=1, replica_groups=mesh['dp'=16,'tensor'=16] {'dp'}, dimensions={1}, use_global_device_ids=true | all-gather | bytes 139264 | tf_op jit(solution)/shard_map/all_gather | solution.py:37
  39.0 2.9 copy.21
  42.0 14.5 %all-to-all-start = ((bf16[4,128,2048]{2,0,1:T(4,128)(2,1)}), bf16[4,128,2048]{2,0,1:T(4,128)(2,1)}, u32[]{:S(2)}, u32[]{:S(2)}) async-start(bf16[4,128,2048]{2,0,1:T(4,128)(2,1)} %copy.21), calls=%async_computation | async-start | bytes 4194304 | tf_op jit(solution)/shard_map/all_to_all | solution.py:23
  56.5 45.4 %all_gather.15 = bf16[4,128,128]{2,1,0:T(8,128)(2,1)S(1)} all-gather(bf16[4,8,128]{2,1,0:T(8,128)(2,1)S(1)} %copy-done.5), channel_id=1, replica_groups=mesh['dp'=16,'tensor'=16] {'dp'}, dimensions={1}, use_global_device_ids=true | all-gather | bytes 139264 | tf_op jit(solution)/shard_map/all_gather | solution.py:40
  101.9 2.3 convolution_convert_fusion.3
  104.2 3.0 copy.30
  107.2 11.8 %all-to-all-start.2 = ((bf16[4,128,2048]{2,0,1:T(4,128)(2,1)}), bf16[4,128,2048]{2,0,1:T(4,128)(2,1)}, u32[]{:S(2)}, u32[]{:S(2)}) async-start(bf16[4,128,2048]{2,0,1:T(4,128)(2,1)} %copy.30), calls=%async_computation.2 | async-start | bytes 4194304 | tf_op jit(solution)/shard_map/all_to_all | solution.py:23
  119.1 46.9 %all_gather.13 = bf16[8,64,256]{2,0,1:T(8,128)(2,1)S(1)} all-gather(bf16[8,4,256]{2,0,1:T(8,128)(2,1)S(1)} %copy.23), channel_id=1, replica_groups=mesh['dp'=16,'tensor'=16] {'dp'}, dimensions={1}, use_global_device_ids=true | all-gather | bytes 278528 | tf_op jit(solution)/shard_map/all_gather | solution.py:38
  166.0 24.3 %all_gather.14 = bf16[8,64,256]{2,0,1:T(8,128)(2,1)S(1)} all-gather(bf16[8,4,256]{2,0,1:T(8,128)(2,1)S(1)} %copy.25), channel_id=1, replica_groups=mesh['dp'=16,'tensor'=16] {'dp'}, dimensions={1}, use_global_device_ids=true | all-gather | bytes 278528 | tf_op jit(solution)/shard_map/all_gather | solution.py:39
  190.3 4.3 copy.80
  194.5 3.9 all_to_all.55
  198.5 4.3 copy.79
  202.7 4.0 all_to_all.63
  206.7 7.5 %fusion.7 = (bf16[8,256,2048]{1,2,0:T(8,128)(2,1)}, f32[8,2048,256]{2,1,0:T(8,128)S(1)}) fusion(bf16[64,8,2048]{2,0,1:T(8,128)(2,1)} %all_to_all.55, bf16[8,64,256]{2,0,1:T(8,128)(2,1)S(1)} %all_gather.13), kind=kOutput, calls=%fused_computation.10 | convolution fusion | flops 557842432 | bytes 27525120 | tf_op jit(solution)/shard_map/kjt,jkm->jmt/dot_general | solution.py:19
  214.2 8.5 %fusion.5 = bf16[8,256,2048]{1,2,0:T(8,128)(2,1)S(1)} fusion(f32[8,2048,256]{2,1,0:T(8,128)S(1)} %get-tuple-element.19, bf16[64,8,2048]{2,0,1:T(8,128)(2,1)S(1)} %copy-done.2, bf16[8,64,256]{2,0,1:T(8,128)(2,1)S(1)} %all_gather.14), kind=kOutput, calls=%fused_computation.6 | convolution fusion | flops 578813952 | bytes 27525120 | tf_op jit(solution)/shard_map/kjt,jkm->jmt/dot_general | solution.py:19
  222.7 2.6 fusion.11
  225.9 2.5 copy.35
  228.4 18.5 %all-to-all-start.3 = ((bf16[64,8,2048]{2,1,0:T(8,128)(2,1)}), bf16[64,8,2048]{2,1,0:T(8,128)(2,1)}, u32[]{:S(2)}, u32[]{:S(2)}) async-start(bf16[64,8,2048]{2,1,0:T(8,128)(2,1)} %copy.35), calls=%async_computation.3 | async-start | bytes 4194304 | tf_op jit(solution)/shard_map/all_to_all | solution.py:27
  247.0 5.5 fusion.30
  253.6 6.0 fusion.10
  259.6 2.5 copy.28
  262.0 14.7 %all-to-all-done.3 = bf16[64,8,2048]{2,1,0:T(8,128)(2,1)} async-done(((bf16[64,8,2048]{2,1,0:T(8,128)(2,1)}), bf16[64,8,2048]{2,1,0:T(8,128)(2,1)}, u32[]{:S(2)}, u32[]{:S(2)}) %all-to-all-start.3) | async-done | bytes 2097184 | tf_op jit(solution)/shard_map/all_to_all | solution.py:27
  276.8 5.2 all-to-all-start.1
  282.2 5.5 fusion.31
  290.2 23.7 %reduce-scatter.4.cloned.1.call-done = f32[8,4,256]{2,0,1:T(8,128)} async-done(((f32[8,64,256]{2,0,1:T(8,128)}), f32[8,4,256]{2,0,1:T(8,128)}) %reduce-scatter.4.cloned.1.call-update) | async-done | bytes 32784 | tf_op jit(solution)/shard_map/reduce_scatter | solution.py:62
  315.3 68.8 %reduce-scatter.6.cloned.1.call-done = f32[8,4,256]{2,0,1:T(8,128)} async-done(((f32[8,64,256]{2,0,1:T(8,128)}), f32[8,4,256]{2,0,1:T(8,128)}) %reduce-scatter.6.cloned.1.call-update) | async-done | bytes 32784 | tf_op jit(solution)/shard_map/reduce_scatter | solution.py:63
  385.5 2.3 fusion.22
  388.7 3.6 fusion.12
  392.4 3.6 convolution_convert_fusion.2
  396.0 3.7 convolution_convert_fusion.4
  399.6 124.9 %all-reduce.3.cloned.1.call-done = f32[4,128,128]{2,0,1:T(4,128)} async-done(((f32[4,128,128]{2,0,1:T(4,128)}), f32[4,128,128]{2,0,1:T(4,128)}) %all-reduce.3.cloned.1.call-update) | async-done | bytes 262160
  525.9 69.5 %reduce-scatter.8.cloned.1.call-done = f32[4,8,128]{2,1,0:T(8,128)} async-done(((f32[4,128,128]{2,1,0:T(8,128)}), f32[4,8,128]{2,1,0:T(8,128)}) %reduce-scatter.8.cloned.1.call-update) | async-done | bytes 16400 | tf_op jit(solution)/shard_map/reduce_scatter | solution.py:64
  (36 shorter events, 9.6 us)
Async XLA Ops:
  7.2 31.1 %copy-start = (bf16[512,2048]{1,0:T(8,128)(2,1)S(1)}, bf16[512,2048]{1,0:T(8,128)(2,1)}, u32[]{:S(2)}) copy-start(bf16[512,2048]{1,0:T(8,128)(2,1)} %param.6) | copy-start | bytes 6291460
  42.0 14.5 %copy-start.5 = (bf16[4,8,128]{2,1,0:T(8,128)(2,1)S(1)}, bf16[4,8,128]{2,1,0:T(8,128)(2,1)}, u32[]{:S(2)}) copy-start(bf16[4,8,128]{2,1,0:T(8,128)(2,1)} %param.11) | copy-start | bytes 24580
  42.0 65.2 %all-to-all-start = ((bf16[4,128,2048]{2,0,1:T(4,128)(2,1)}), bf16[4,128,2048]{2,0,1:T(4,128)(2,1)}, u32[]{:S(2)}, u32[]{:S(2)}) async-start(bf16[4,128,2048]{2,0,1:T(4,128)(2,1)} %copy.21), calls=%async_computation | async-start | bytes 4194304 | tf_op jit(solution)/shard_map/all_to_all | solution.py:23
  107.2 11.8 %copy-start.3 = (bf16[8,4,256]{2,1,0:T(4,128)(2,1)S(1)}, bf16[8,4,256]{2,1,0:T(4,128)(2,1)}, u32[]{:S(2)}) copy-start(bf16[8,4,256]{2,1,0:T(4,128)(2,1)} %param.9) | copy-start | bytes 49156
  107.2 11.8 %copy-start.4 = (bf16[8,4,256]{2,1,0:T(4,128)(2,1)S(1)}, bf16[8,4,256]{2,1,0:T(4,128)(2,1)}, u32[]{:S(2)}) copy-start(bf16[8,4,256]{2,1,0:T(4,128)(2,1)} %param.10) | copy-start | bytes 49156
  107.2 91.3 %all-to-all-start.2 = ((bf16[4,128,2048]{2,0,1:T(4,128)(2,1)}), bf16[4,128,2048]{2,0,1:T(4,128)(2,1)}, u32[]{:S(2)}, u32[]{:S(2)}) async-start(bf16[4,128,2048]{2,0,1:T(4,128)(2,1)} %copy.30), calls=%async_computation.2 | async-start | bytes 4194304 | tf_op jit(solution)/shard_map/all_to_all | solution.py:23
  206.7 7.5 %copy-start.2 = (bf16[64,8,2048]{2,0,1:T(8,128)(2,1)S(1)}, bf16[64,8,2048]{2,0,1:T(8,128)(2,1)}, u32[]{:S(2)}) copy-start(bf16[64,8,2048]{2,0,1:T(8,128)(2,1)} %all_to_all.63) | copy-start | bytes 6291460
  222.7 3.2 copy-start.1
  228.4 48.3 %all-to-all-start.3 = ((bf16[64,8,2048]{2,1,0:T(8,128)(2,1)}), bf16[64,8,2048]{2,1,0:T(8,128)(2,1)}, u32[]{:S(2)}, u32[]{:S(2)}) async-start(bf16[64,8,2048]{2,1,0:T(8,128)(2,1)} %copy.35), calls=%async_computation.3 | async-start | bytes 4194304 | tf_op jit(solution)/shard_map/all_to_all | solution.py:27
  246.9 66.9 %reduce-scatter.4.cloned.1.call-start = ((), (), s32[]{:S(2)}) async-start(), calls=%async_computation.7 | async-start | bytes 557056 | tf_op jit(solution)/shard_map/reduce_scatter | solution.py:62
  276.8 111.9 %all-to-all-start.1 = ((bf16[64,8,2048]{2,1,0:T(8,128)(2,1)}), bf16[64,8,2048]{2,1,0:T(8,128)(2,1)}, u32[]{:S(2)}, u32[]{:S(2)}) async-start(bf16[64,8,2048]{2,1,0:T(8,128)(2,1)} %copy.28), calls=%async_computation.1 | async-start | bytes 4194304 | tf_op jit(solution)/shard_map/all_to_all | solution.py:27
  281.9 7.0 %copy-start.6 = (u32[256]{0:T(256)S(1)}, u32[256]{0:T(256)}, u32[]{:S(2)}) copy-start(u32[256]{0:T(256)} %constant.16) | copy-start | bytes 3076
  281.9 102.1 %reduce-scatter.6.cloned.1.call-start = ((), (), s32[]{:S(2)}) async-start(), calls=%async_computation.8 | async-start | bytes 557056 | tf_op jit(solution)/shard_map/reduce_scatter | solution.py:63
  288.9 235.7 %all-reduce.3.cloned.1.call-start = ((), (), s32[]{:S(2)}) async-start(), calls=%async_computation.10 | async-start | bytes 524288
  388.7 206.7 %reduce-scatter.8.cloned.1.call-start = ((), (), s32[]{:S(2)}) async-start(), calls=%async_computation.9 | async-start | bytes 278528 | tf_op jit(solution)/shard_map/reduce_scatter | solution.py:64
Sparse Core Ops, SparseCore 0:
  253.7 60.1 reduce-scatter.3
  316.5 67.5 reduce-scatter.5
  388.8 135.7 all-reduce.2
  527.6 67.6 reduce-scatter.7
where the time goes:
time: 614 us; the launch traced here: 602 us
  waiting for transfers between devices  302 us (49%)
  blocking collectives  148 us (24%)
  matrix products  51.8 us (8%)
  starting transfers between devices  50.4 us (8%)
  local copies, waits for them, and re-layouts  35.7 us (6%)
  between operations  14.5 us (2%)
    unnamed x5, waiting for transfers between devices  125 us
    reduce_scatter x1, waiting for transfers between devices, local(): lax.psum_scatter(part_r2, 'dp', scatter_dimension=1, tiled=True)  69.5 us
    reduce_scatter x1, waiting for transfers between devices, local(): lax.psum_scatter(part_l2, 'dp', scatter_dimension=1, tiled=True)  68.8 us
    dot_general x12, matrix products, product(): return jnp.einsum(form, left, right, preferred_element_type=jnp.float32)  51.8 us
    all_gather x1, blocking collectives, local(): lax.all_gather(second_up, 'dp', axis=1, tiled=True)  46.9 us
    all_gather x1, blocking collectives, local(): lax.all_gather(first_down, 'dp', axis=1, tiled=True)  45.4 us
    all_gather x1, blocking collectives, local(): lax.all_gather(first_up, 'dp', axis=1, tiled=True)  31.1 us
    all_to_all x2, starting transfers between devices, transpose_blocks(): lax.all_to_all(values, 'tensor', split_axis=1, concat_axis=0, tiled=True)  26.4 us
  transfers between devices with their start and end apart: 8, of which 5 were waited for; matrix products, arithmetic and copies ran while one was open for 8% of the time, Pallas kernels for 0%

commit v1 on v0

v1 whole, which is shorter than its diff:
```python
import jax
import jax.numpy as jnp
from jax import lax
from jax.experimental import pallas as pl
from jax.experimental.pallas import tpu as pltpu
from jax.sharding import PartitionSpec as P

BF = jnp.bfloat16
F32 = jnp.float32
N = 16
NC = 4
TC = 512
NT = (((1,), (1,)), ((), ()))
TN = (((0,), (1,)), ((), ()))


def mm(a, b):
    return jnp.dot(a, b, preferred_element_type=F32)


def mm_nt(a, b):
    return lax.dot_general(a, b, NT, preferred_element_type=F32)


def iota(shape, dim):
    return lax.broadcasted_iota(jnp.int32, shape, dim)


def each(count, body):
    lax.fori_loop(0, count, lambda i, c: (body(i), c)[1], 0)


def kernel(
    x_hbm, g_hbm, au_hbm, ad_hbm, bu_hbm, bd_hbm,
    out_hbm, gin_hbm, r1_ref, l1_ref, l2_ref, r2_ref,
    xv, gv, au, ad, bu, bd, wau, wad, wcu, wcd, wbu, wbd, wtu, wtd,
    s1s, b3s, s1r, b3r, s3s, bos, s3r, bor, hid, slope, bp, outv, ginv,
    lacc, r1acc, r2acc, lrecv, r1recv, r2recv, r2sum,
    ag_send, ag_recv, a2a_send, a2a_recv, rs_send, rs_recv, load_sem, store_sem,
):
    me_dp = lax.axis_index("dp")
    me_tn = lax.axis_index("tensor")

    def dp_peer(r):
        return (lax.rem(me_dp + r, N), me_tn)

    def tn_peer(r):
        return (me_dp, lax.rem(me_tn + r, N))

    def load(c):
        at = pl.ds(pl.multiple_of(c * TC, TC), TC)
        return (
            pltpu.make_async_copy(x_hbm.at[:, at], xv.at[c], load_sem.at[0, c]),
            pltpu.make_async_copy(g_hbm.at[:, at], gv.at[c], load_sem.at[1, c]),
        )

    def start_load(c):
        for copy in load(c):
            copy.start()

    each(NC, start_load)

    barrier = pltpu.get_barrier_semaphore()

    def greet(r):
        pl.semaphore_signal(barrier, inc=1, device_id=dp_peer(r + 1), device_id_type=pl.DeviceIdType.MESH)
        pl.semaphore_signal(barrier, inc=1, device_id=tn_peer(r + 1), device_id_type=pl.DeviceIdType.MESH)

    each(N - 1, greet)
    pl.semaphore_wait(barrier, 2 * (N - 1))

    def remote(src, dst, send, recv, peer):
        pltpu.make_async_remote_copy(
            src_ref=src, dst_ref=dst, send_sem=send, recv_sem=recv,
            device_id=peer, device_id_type=pl.DeviceIdType.MESH,
        ).start()

    def wait_bytes(ref, sem):
        pltpu.make_async_copy(ref, ref, sem).wait()

    gathers = ((au_hbm, au), (ad_hbm, ad), (bu_hbm, bu), (bd_hbm, bd))
    for n, (shard, whole) in enumerate(gathers):
        pltpu.make_async_copy(shard, whole.at[:, me_dp], ag_recv.at[n]).start()

        def gather_send(r, n=n, shard=shard, whole=whole):
            remote(shard, whole.at[:, me_dp], ag_send.at[n], ag_recv.at[n], dp_peer(r + 1))

        each(N - 1, gather_send)

    def spread(k):
        return (iota((512, 128), 0) == 4 * iota((512, 128), 1) + k).astype(BF)

    def square(ref, k):
        return ref[k].astype(F32).reshape(128, 128).astype(BF)

    wait_bytes(au, ag_recv.at[0])
    for k in range(4):
        rows = pl.ds(128 * k, 128)
        block = square(au, k)
        wau[:, rows] = mm_nt(spread(k), block).astype(BF)
        wcu[rows, :] = mm_nt(block, spread(k)).astype(BF)
    wait_bytes(ad, ag_recv.at[1])
    for k in range(4):
        rows = pl.ds(128 * k, 128)
        block = square(ad, k)
        wad[:, rows] = mm(spread(k), block).astype(BF)
        wcd[rows, :] = lax.dot_general(block, spread(k), TN, preferred_element_type=F32).astype(BF)

    def exchange_out(c, kind, src, dst):
        def one(r):
            to = lax.rem(me_tn + r + 1, N)
            remote(src.at[c, to], dst.at[c, :, me_tn], a2a_send.at[kind], a2a_recv.at[kind, c], (me_dp, to))

        each(N - 1, one)
        pltpu.make_async_copy(src.at[c, me_tn], dst.at[c, :, me_tn], a2a_recv.at[kind, c]).start()

    def exchange_back(c, kind, src, dst):
        def one(r):
            to = lax.rem(me_tn + r + 1, N)
            remote(src.at[c, :, to], dst.at[c, me_tn], a2a_send.at[kind], a2a_recv.at[kind, c], (me_dp, to))

        each(N - 1, one)
        pltpu.make_async_copy(src.at[c, :, me_tn], dst.at[c, me_tn], a2a_recv.at[kind, c]).start()

    def stage_a(c):
        copy_x, copy_g = load(c)
        copy_x.wait()
        s1s[c] = mm(wau[...], xv[c]).astype(BF).reshape(N, 2, 16, TC)
        exchange_out(c, 0, s1s, s1r)
        copy_g.wait()
        b3s[c] = mm(wad[...], gv[c]).astype(BF).reshape(N, 2, 16, TC)
        exchange_out(c, 1, b3s, b3r)

    each(NC, stage_a)

    for n, (whole, wide, tall) in enumerate(((bu, wtu, wbu), (bd, wtd, wbd))):
        wait_bytes(whole, ag_recv.at[2 + n])
        for q in range(2):
            block = whole[q].reshape(256, 256)
            flipped = block.astype(F32).T.astype(BF)
            zero = jnp.zeros_like(block)
            row_j = lax.rem(iota((256, 256), 0) // 4, 4)
            col_j = lax.rem(iota((256, 256), 1) // 4, 4)
            for b in range(4):
                wide[q, :, pl.ds(256 * b, 256)] = jnp.where(row_j == b, block, zero)
                tall[q, b] = jnp.where(col_j == b, flipped, zero)

    lacc[...] = jnp.zeros_like(lacc)
    r1acc[...] = jnp.zeros_like(r1acc)
    r2acc[...] = jnp.zeros_like(r2acc)

    def stage_b(c):
        wait_bytes(s1r.at[c], a2a_recv.at[0, c])

        def forward(q):
            moved = s1r[c, q].reshape(256, TC)

            def block(b):
                pre = mm(wbu[q, b], moved)
                half = 0.5 * (1.0 + lax.erf(pre * 0.7071067811865476))
                rows = pl.ds(pl.multiple_of(256 * b, 256), 256)
                hid[q, rows, :] = (pre * half).astype(BF)
                slope[q, rows, :] = half + pre * jnp.exp(-0.5 * pre * pre) * 0.3989422804014327

            each(4, block)
            s3s[c, q] = mm(wtd[q], hid[q]).astype(BF).reshape(N, 16, TC)

        each(2, forward)
        exchange_back(c, 2, s3s, s3r)
        wait_bytes(b3r.at[c], a2a_recv.at[1, c])

        def backward(q):
            moved = s1r[c, q].reshape(256, TC)
            back = b3r[c, q].reshape(256, TC)
            row_j = lax.rem(iota((256, 256), 0) // 4, 4)

            def block(b):
                rows = pl.ds(pl.multiple_of(256 * b, 256), 256)
                grad = (mm(wbd[q, b], back) * slope[q, rows, :]).astype(BF)
                bp[rows, :] = grad
                part_one = jnp.where(row_j == b, mm_nt(moved, grad), 0.0)
                part_two = jnp.where(row_j == b, mm_nt(back, hid[q, rows, :]), 0.0)
                lacc[0, q] += part_one.reshape(N, 16, 256)
                lacc[1, q] += part_two.reshape(N, 16, 256)

            each(4, block)
            bos[c, q] = mm(wtu[q], bp[...]).astype(BF).reshape(N, 16, TC)

        each(2, backward)
        exchange_back(c, 3, bos, bor)

    each(NC, stage_b)

    def reduce_out(n, src, dst, at):
        def one(r):
            to = lax.rem(me_dp + r + 1, N)
            remote(at(src, to), dst.at[me_dp], rs_send.at[n], rs_recv.at[n], (to, me_tn))

        each(N - 1, one)
        pltpu.make_async_copy(at(src, me_dp), dst.at[me_dp], rs_recv.at[n]).start()

    def reduce_in(n, ref):
        wait_bytes(ref, rs_recv.at[n])
        total = ref[0]
        for d in range(1, N):
            total = total + ref[d]
        return total

    reduce_out(0, lacc, lrecv, lambda ref, to: ref.at[:, :, to])

    def store(c):
        at = pl.ds(pl.multiple_of(c * TC, TC), TC)
        return (
            pltpu.make_async_copy(outv.at[c], out_hbm.at[:, at], store_sem.at[0, c]),
            pltpu.make_async_copy(ginv.at[c], gin_hbm.at[:, at], store_sem.at[1, c]),
        )

    def stage_c_out(c):
        wait_bytes(s3r.at[c], a2a_recv.at[2, c])
        moved = s3r[c].reshape(512, TC)
        outv[c] = mm(wcd[...], moved).astype(BF)
        store(c)[0].start()
        row_k = lax.rem(iota((512, 128), 0), 4)
        for p in range(2):
            part = mm_nt(moved, gv[c, pl.ds(256 * p, 256), :])
            part = jnp.where(row_k == 2 * p, part[:, :128], jnp.where(row_k == 2 * p + 1, part[:, 128:], 0.0))
            r2acc[...] += part.reshape(N, 32, 128)

    def stage_c_in(c):
        wait_bytes(bor.at[c], a2a_recv.at[3, c])
        moved = bor[c].reshape(512, TC)
        col_k = lax.rem(iota((128, 512), 1), 4)
        for p in range(2):
            part = mm_nt(xv[c, pl.ds(256 * p, 256), :], moved)
            part = jnp.where(col_k == 2 * p, part[:128], jnp.where(col_k == 2 * p + 1, part[128:], 0.0))
            r1acc[...] += part.reshape(N, 8, 512)
        ginv[c] = mm(wcu[...], moved).astype(BF)
        store(c)[1].start()

    def stage_c(c):
        stage_c_out(c)

        @pl.when(c == NC - 1)
        def _():
            reduce_out(1, r2acc, r2recv, lambda ref, to: ref.at[to])

        stage_c_in(c)

    each(NC, stage_c)
    reduce_out(2, r1acc, r1recv, lambda ref, to: ref.at[to])

    total = reduce_in(0, lrecv)
    l1_ref[...] = total[0]
    l2_ref[...] = total[1]
    r2sum[...] = reduce_in(1, r2recv)
    for k in range(4):
        r2_ref[k] = r2sum[pl.ds(k, 8, stride=4), :]
    total = reduce_in(2, r1recv)
    for k in range(4):
        r1_ref[k] = jnp.dot(total, spread(k).astype(F32), preferred_element_type=F32, precision=lax.Precision.HIGHEST)

    def finish(c):
        for copy in store(c):
            copy.wait()

    each(NC, finish)
    for n, (_, whole) in enumerate(gathers):
        wait_bytes(whole.at[:, pl.ds(0, N - 1)], ag_send.at[n])
    wait_bytes(s1s.at[:, pl.ds(0, N - 1)], a2a_send.at[0])
    wait_bytes(b3s.at[:, pl.ds(0, N - 1)], a2a_send.at[1])
    wait_bytes(s3s.at[:, :, pl.ds(0, N - 1)], a2a_send.at[2])
    wait_bytes(bos.at[:, :, pl.ds(0, N - 1)], a2a_send.at[3])
    wait_bytes(lrecv.at[pl.ds(0, N - 1)], rs_send.at[0])
    wait_bytes(r2recv.at[pl.ds(0, N - 1)], rs_send.at[1])
    wait_bytes(r1recv.at[pl.ds(0, N - 1)], rs_send.at[2])


def local(activations, cotangent, first_up, second_up, second_down, first_down):
    any_spec = pl.BlockSpec(memory_space=pl.ANY)
    vmem = pl.BlockSpec(memory_space=pltpu.VMEM)
    scratch = [
        pltpu.VMEM((NC, 512, TC), BF),
        pltpu.VMEM((NC, 512, TC), BF),
        pltpu.VMEM((4, N, 8, 128), BF),
        pltpu.VMEM((4, N, 8, 128), BF),
        pltpu.VMEM((2, N, 16, 256), BF),
        pltpu.VMEM((2, N, 16, 256), BF),
        pltpu.VMEM((512, 512), BF),
        pltpu.VMEM((512, 512), BF),
        pltpu.VMEM((512, 512), BF),
        pltpu.VMEM((512, 512), BF),
        pltpu.VMEM((2, 4, 256, 256), BF),
        pltpu.VMEM((2, 4, 256, 256), BF),
        pltpu.VMEM((2, 256, 1024), BF),
        pltpu.VMEM((2, 256, 1024), BF),
        pltpu.VMEM((NC, N, 2, 16, TC), BF),
        pltpu.VMEM((NC, N, 2, 16, TC), BF),
        pltpu.VMEM((NC, 2, N, 16, TC), BF),
        pltpu.VMEM((NC, 2, N, 16, TC), BF),
        pltpu.VMEM((NC, 2, N, 16, TC), BF),
        pltpu.VMEM((NC, 2, N, 16, TC), BF),
        pltpu.VMEM((NC, N, 2, 16, TC), BF),
        pltpu.VMEM((NC, N, 2, 16, TC), BF),
        pltpu.VMEM((2, 1024, TC), BF),
        pltpu.VMEM((2, 1024, TC), F32),
        pltpu.VMEM((1024, TC), BF),
        pltpu.VMEM((NC, 512, TC), BF),
        pltpu.VMEM((NC, 512, TC), BF),
        pltpu.VMEM((2, 2, N, 16, 256), F32),
        pltpu.VMEM((N, 8, 512), F32),
        pltpu.VMEM((N, 32, 128), F32),
        pltpu.VMEM((N, 2, 2, 16, 256), F32),
        pltpu.VMEM((N, 8, 512), F32),
        pltpu.VMEM((N, 32, 128), F32),
        pltpu.VMEM((32, 128), F32),
        pltpu.SemaphoreType.DMA((4,)),
        pltpu.SemaphoreType.DMA((4,)),
        pltpu.SemaphoreType.DMA((4,)),
        pltpu.SemaphoreType.DMA((4, NC)),
        pltpu.SemaphoreType.DMA((3,)),
        pltpu.SemaphoreType.DMA((3,)),
        pltpu.SemaphoreType.DMA((2, NC)),
        pltpu.SemaphoreType.DMA((2, NC)),
    ]
    out, gin, r1, l1, l2, r2 = pl.pallas_call(
        kernel,
        name="monarch_layer",
        out_shape=(
            jax.ShapeDtypeStruct((512, 2048), BF),
            jax.ShapeDtypeStruct((512, 2048), BF),
            jax.ShapeDtypeStruct((4, 8, 128), F32),
            jax.ShapeDtypeStruct((2, 16, 256), F32),
            jax.ShapeDtypeStruct((2, 16, 256), F32),
            jax.ShapeDtypeStruct((4, 8, 128), F32),
        ),
        in_specs=[any_spec] * 6,
        out_specs=(any_spec, any_spec, vmem, vmem, vmem, vmem),
        scratch_shapes=scratch,
        compiler_params=pltpu.CompilerParams(
            collective_id=0, has_side_effects=True, vmem_limit_bytes=60 * 1024 * 1024
        ),
    )(
        activations, cotangent, first_up, first_down,
        second_up.reshape(2, 16, 256), second_down.reshape(2, 16, 256),
    )
    return out, gin, r1, l1.reshape(8, 4, 256), l2.reshape(8, 4, 256), r2


def solution(mesh):
    spec = (P("tensor", "dp"),) * 2 + (P("tensor", "dp", None),) * 4
    return jax.shard_map(local, mesh=mesh, in_specs=spec, out_specs=spec, check_vma=False)
```

time: 614 us -> 150 us (0.24); the launches traced: 602 us -> 150 us
  waiting for transfers between devices: 302 us -> 0 us
  blocking collectives: 148 us -> 0 us
  Pallas kernels: 0 us -> 138 us
  matrix products: 51.8 us -> 0 us
  starting transfers between devices: 50.4 us -> 0 us
  local copies, waits for them, and re-layouts: 35.7 us -> 11.3 us
  between operations: 14.5 us -> 0.65 us
    reduce_scatter x3 -> x0, waiting for transfers between devices: 162 us -> none  [the longest x1 69.5 us: local(): lax.psum_scatter(part_r2, 'dp', scatter_dimension=1, tiled=True)]
    all_gather x4 -> x0, blocking collectives: 148 us -> none  [the longest x1 46.9 us: local(): lax.all_gather(second_up, 'dp', axis=1, tiled=True)]
    pallas_call x0 -> x1, Pallas kernels: none -> 138 us  [local(): pl.pallas_call(kernel, name='monarch_layer', out_shape=(jax.ShapeDtypeStr...]
    unnamed x5 -> x0, waiting for transfers between devices: 125 us -> none
    dot_general x12 -> x0, matrix products: 51.8 us -> none  [product(): return jnp.einsum(form, left, right, preferred_element_type=jnp.float32)]
    all_to_all x4 -> x0, starting transfers between devices: 50 us -> none  [the longest x2 26.4 us: transpose_blocks(): lax.all_to_all(values, 'tensor', split_axis=1, concat_axis=0, tiled=True)]
    all_to_all x4 -> x0, local copies, waits for them, and re-layouts: 16.5 us -> none  [transpose_blocks(): lax.all_to_all(values, 'tensor', split_axis=1, concat_axis=0, tiled=True)]
    all_to_all x4 -> x0, waiting for transfers between devices: 14.7 us -> none  [the longest x2 14.7 us: restore_blocks(): lax.all_to_all(values, 'tensor', split_axis=0, concat_axis=1, tiled=True)]
  transfers between devices with their start and end apart: 8 -> 0, of which waited for: 5 -> 0; matrix products, arithmetic and copies ran while one was open for 8% -> 0% of each run, Pallas kernels for 0% -> 0%
where the time goes in v1:
time: 150 us
  Pallas kernels  138 us (92%)
  local copies, waits for them, and re-layouts  11.3 us (8%)
    pallas_call x1, Pallas kernels, local(): pl.pallas_call(kernel, name='monarch_layer', out_shape=(jax.ShapeDtypeStr...  138 us
    unnamed x10, local copies, waits for them, and re-layouts  5.85 us

profile of v1, /device:TPU:1, one launch (start us, length us, event | category | flops | bytes accessed | tf_op | source)
XLA Modules:
  0.0 149.8 jit_solution(12764137571013033950)
XLA Ops:
  0.6 1.3 reshape.24.bu_hbm
  2.0 1.3 reshape.25.bd_hbm
  3.3 137.8 %monarch_layer.1 = (bf16[512,2048]{1,0:T(8,128)(2,1)}, bf16[512,2048]{1,0:T(8,128)(2,1)}, f32[4,8,128]{2,1,0:T(8,128)}, f32[2,16,256]{2,1,0:T(8,128)}, f32[2,16,256]{2,1,0:T(8,128)}, /*index=5*/f32[4,8,128]{2,1,0:T(8,128)}) custom-call(bf16[512,2048]{1,0:T(8,128)(2,1)} %x_hbm.1, bf16[512,2048]{1,0:T(8,128)(2,1)} %g_hbm.1, bf16[4,8,128]{2,1,0:T(8,128)(2,1)} %au_hbm.1, ...), custom_call_target="tpu_custom_call" | custom-call | tf_op jit(solution)/shard_map/monarch_layer/pallas_call | solution.py:325
  141.1 1.4 reshape.26
  142.5 1.4 reshape.27
  143.9 0.0 copy-start
  143.9 3.3 %copy.16 = bf16[512,2048]{1,0:T(8,128)(2,1)} copy(bf16[512,2048]{1,0:T(8,128)(2,1)} %get-tuple-element.24) | data formatting | bytes 4194304
  147.2 0.0 copy-done
  147.2 0.0 copy-start.2
  147.2 0.0 copy-start.1
  147.2 1.3 copy.17
  148.5 0.0 copy-done.2
  148.5 0.6 copy.18
  149.1 0.0 copy-done.1
  149.1 0.6 copy.19
Async XLA Ops:
  143.9 3.3 %copy-start = (bf16[512,2048]{1,0:T(8,128)(2,1)S(1)}, bf16[512,2048]{1,0:T(8,128)(2,1)}, u32[]{:S(2)}) copy-start(bf16[512,2048]{1,0:T(8,128)(2,1)} %get-tuple-element.25) | copy-start | bytes 6291460
  147.2 1.3 copy-start.2
  147.2 1.9 %copy-start.1 = (f32[4,8,128]{2,1,0:T(8,128)S(1)}, f32[4,8,128]{2,1,0:T(8,128)}, u32[]{:S(2)}) copy-start(f32[4,8,128]{2,1,0:T(8,128)} %get-tuple-element.29) | copy-start | bytes 49156

commit v2 on v1

v2 whole, which is shorter than its diff:
```python
import jax
import jax.numpy as jnp
from jax import lax
from jax.experimental import pallas as pl
from jax.experimental.pallas import tpu as pltpu
from jax.sharding import PartitionSpec as P

BF = jnp.bfloat16
F32 = jnp.float32
N = 16
NZ = 8
NC = 4
TC = 512
B_SHAPE = (2, 4, 4, 256)
L_SHAPE = (8, 4, 256)
NT = (((1,), (1,)), ((), ()))
TN = (((0,), (1,)), ((), ()))


def mm(a, b):
    return jnp.dot(a, b, preferred_element_type=F32)


def mm_nt(a, b):
    return lax.dot_general(a, b, NT, preferred_element_type=F32)


def iota(shape, dim):
    return lax.broadcasted_iota(jnp.int32, shape, dim)


def each(count, body):
    lax.fori_loop(0, count, lambda i, c: (body(i), c)[1], 0)


def kernel(
    x_hbm, g_hbm, au_hbm, ad_hbm, bu_hbm, bd_hbm,
    out_hbm, gin_hbm, r1_ref, l1_ref, l2_ref, r2_ref,
    xv, gv, au, ad, bu, bd, wau, wad, wcu, wcd, wbu, wbd, wtu, wtd,
    s1s, b3s, s1r, b3r, s3s, bos, s3r, bor, hid, slope, bp, outv, ginv,
    lacc, r1acc, r2acc, lrecv, r1recv, r2recv, lsum, r2sum, lpair, r2pair, r2rows,
    ag_send, ag_recv, pair_recv, a2a_send, a2a_recv, rs_send, rs_recv, half_send, half_recv,
    load_sem, store_sem,
):
    me_dp = lax.axis_index("dp")
    me_tn = lax.axis_index("tensor")
    me_z = me_dp // 2
    me_xl = lax.rem(me_dp, 2)
    pair = 2 * me_z + 1 - me_xl

    def load(c):
        at = pl.ds(pl.multiple_of(c * TC, TC), TC)
        return (
            pltpu.make_async_copy(x_hbm.at[:, at], xv.at[c], load_sem.at[0, c]),
            pltpu.make_async_copy(g_hbm.at[:, at], gv.at[c], load_sem.at[1, c]),
        )

    barrier = pltpu.get_barrier_semaphore()

    def greet(r):
        for peer in ((lax.rem(me_dp + r + 1, N), me_tn), (me_dp, lax.rem(me_tn + r + 1, N))):
            pl.semaphore_signal(barrier, inc=1, device_id=peer, device_id_type=pl.DeviceIdType.MESH)

    each(N - 1, greet)

    def start_load(c):
        copy_x, copy_g = load(c)
        copy_x.start()
        copy_g.start()

    each(NC, start_load)
    pl.semaphore_wait(barrier, 2 * (N - 1))

    def remote(src, dst, send, recv, peer):
        pltpu.make_async_remote_copy(
            src_ref=src, dst_ref=dst, send_sem=send, recv_sem=recv,
            device_id=peer, device_id_type=pl.DeviceIdType.MESH,
        ).start()

    def wait_bytes(ref, sem):
        pltpu.make_async_copy(ref, ref, sem).wait()

    first = ((au_hbm, au), (ad_hbm, ad))
    for n, (shard, whole) in enumerate(first):
        def gather_send(r, n=n, shard=shard, whole=whole):
            remote(shard, whole.at[:, me_dp], ag_send.at[n], ag_recv.at[n], (lax.rem(me_dp + r + 1, N), me_tn))

        each(N - 1, gather_send)
        pltpu.make_async_copy(shard, whole.at[:, me_dp], ag_recv.at[n]).start()

    second = ((bu_hbm, bu), (bd_hbm, bd))
    for n, (shard, whole) in enumerate(second):
        remote(shard, whole.at[:, me_dp], ag_send.at[2 + n], pair_recv.at[n], (pair, me_tn))

        def along_z(r, n=n, shard=shard, whole=whole):
            to = 2 * lax.rem(me_z + r + 1, NZ) + me_xl
            remote(shard, whole.at[:, me_dp], ag_send.at[2 + n], ag_recv.at[2 + n], (to, me_tn))

        each(NZ - 1, along_z)
        pltpu.make_async_copy(shard, whole.at[:, me_dp], ag_recv.at[2 + n]).start()

    def pass_on():
        for n, (_, whole) in enumerate(second):
            wait_bytes(whole.at[:, pair], pair_recv.at[n])

            def along_z(r, n=n, whole=whole):
                to = 2 * lax.rem(me_z + r + 1, NZ) + me_xl
                remote(whole.at[:, pair], whole.at[:, pair], ag_send.at[2 + n], ag_recv.at[2 + n], (to, me_tn))

            each(NZ - 1, along_z)

    def spread(k):
        row = iota((512, 128), 0)
        j = 8 * lax.rem(row // 16, N) + 4 * (row // 256) + lax.rem(row // 4, 4)
        return jnp.logical_and(lax.rem(row, 4) == k, iota((512, 128), 1) == j).astype(BF)

    def square(ref, k):
        return ref[k].astype(F32).reshape(128, 128).astype(BF)

    def exchange(c, kind, src, dst):
        def one(r):
            to = lax.rem(me_tn + r + 1, N)
            remote(src.at[c, :, to], dst.at[c, :, me_tn], a2a_send.at[kind], a2a_recv.at[kind, c], (me_dp, to))

        each(N - 1, one)
        pltpu.make_async_copy(src.at[c, :, me_tn], dst.at[c, :, me_tn], a2a_recv.at[kind, c]).start()

    def exchange_half(c, q, src, dst):
        def one(r):
            to = lax.rem(me_tn + r + 1, N)
            remote(src.at[c, q, to], dst.at[c, q, me_tn], a2a_send.at[3], a2a_recv.at[3 + q, c], (me_dp, to))

        each(N - 1, one)
        pltpu.make_async_copy(src.at[c, q, me_tn], dst.at[c, q, me_tn], a2a_recv.at[3 + q, c]).start()

    def stage_a_up(c):
        load(c)[0].wait()
        s1s[c] = mm(wau[...], xv[c]).astype(BF).reshape(2, N, 16, TC)
        exchange(c, 0, s1s, s1r)

    def stage_a_down(c):
        load(c)[1].wait()
        b3s[c] = mm(wad[...], gv[c]).astype(BF).reshape(2, N, 16, TC)
        exchange(c, 1, b3s, b3r)

    wait_bytes(au, ag_recv.at[0])
    for k in range(4):
        wau[:, pl.ds(128 * k, 128)] = mm_nt(spread(k), square(au, k)).astype(BF)
    stage_a_up(0)
    wait_bytes(ad, ag_recv.at[1])
    for k in range(4):
        wad[:, pl.ds(128 * k, 128)] = mm(spread(k), square(ad, k)).astype(BF)
    stage_a_down(0)
    pass_on()

    def stage_a(c):
        stage_a_up(c + 1)
        stage_a_down(c + 1)

    each(NC - 1, stage_a)
    for k in range(4):
        rows = pl.ds(128 * k, 128)
        wcu[rows, :] = mm_nt(square(au, k), spread(k)).astype(BF)
        wcd[rows, :] = lax.dot_general(square(ad, k), spread(k), TN, preferred_element_type=F32).astype(BF)

    for n, (whole, wide, tall) in enumerate(((bu, wtu, wbu), (bd, wtd, wbd))):
        wait_bytes(whole.at[:, pl.ds(0, N - 1)], ag_recv.at[2 + n])
        for q in range(2):
            block = whole[q].reshape(256, 256)
            flipped = block.astype(F32).T.astype(BF)
            zero = jnp.zeros_like(block)
            row_j = lax.rem(iota((256, 256), 0) // 4, 4)
            col_j = lax.rem(iota((256, 256), 1) // 4, 4)
            for b in range(4):
                wide[q, :, pl.ds(256 * b, 256)] = jnp.where(row_j == b, block, zero)
                tall[q, b] = jnp.where(col_j == b, flipped, zero)

    lacc[...] = jnp.zeros_like(lacc)
    r1acc[...] = jnp.zeros_like(r1acc)
    r2acc[...] = jnp.zeros_like(r2acc)

    def stage_b(c):
        wait_bytes(s1r.at[c], a2a_recv.at[0, c])

        def forward(q):
            moved = s1r[c, q].reshape(256, TC)

            def block(b):
                pre = mm(wbu[q, b], moved)
                half = 0.5 * (1.0 + lax.erf(pre * 0.7071067811865476))
                rows = pl.ds(pl.multiple_of(256 * b, 256), 256)
                hid[q, rows, :] = (pre * half).astype(BF)
                slope[q, rows, :] = half + pre * jnp.exp(-0.5 * pre * pre) * 0.3989422804014327

            each(4, block)
            s3s[c, q] = mm(wtd[q], hid[q]).astype(BF).reshape(N, 16, TC)

        each(2, forward)
        exchange(c, 2, s3s, s3r)
        wait_bytes(b3r.at[c], a2a_recv.at[1, c])

        def backward(q):
            moved = s1r[c, q].reshape(256, TC)
            back = b3r[c, q].reshape(256, TC)
            row_j = lax.rem(iota((256, 256), 0) // 4, 4)

            def slopes(b):
                rows = pl.ds(pl.multiple_of(256 * b, 256), 256)
                bp[rows, :] = (mm(wbd[q, b], back) * slope[q, rows, :]).astype(BF)

            each(4, slopes)
            bos[c, q] = mm(wtu[q], bp[...]).astype(BF).reshape(N, 16, TC)
            exchange_half(c, q, bos, bor)

            def sums(b):
                rows = pl.ds(pl.multiple_of(256 * b, 256), 256)
                part_one = jnp.where(row_j == b, mm_nt(moved, bp[rows, :]), 0.0)
                part_two = jnp.where(row_j == b, mm_nt(back, hid[q, rows, :]), 0.0)
                lacc[q] += part_one.reshape(NZ, 2, 16, 256)
                lacc[2 + q] += part_two.reshape(NZ, 2, 16, 256)

            each(4, sums)

        each(2, backward)

    each(NC, stage_b)

    def sum_z_out(n, acc, recv):
        def one(r):
            to = lax.rem(me_z + r + 1, NZ)
            remote(acc.at[:, to], recv.at[me_z], rs_send.at[n], rs_recv.at[n], (2 * to + me_xl, me_tn))

        each(NZ - 1, one)
        pltpu.make_async_copy(acc.at[:, me_z], recv.at[me_z], rs_recv.at[n]).start()

    def sum_z_in(n, recv, sums, pair_ref):
        wait_bytes(recv, rs_recv.at[n])
        for h in range(2):
            total = recv[0, :, h]
            for d in range(1, NZ):
                total = total + recv[d, :, h]
            sums[h] = total
        remote(sums.at[1 - me_xl], pair_ref, half_send.at[n], half_recv.at[n], (pair, me_tn))

    def sum_pair(n, sums, pair_ref):
        wait_bytes(pair_ref, half_recv.at[n])
        return sums[me_xl] + pair_ref[...]

    def sum_out(n, src, dst):
        def one(r):
            to = lax.rem(me_dp + r + 1, N)
            remote(src.at[n, to], dst.at[n, me_dp], rs_send.at[2 + n], rs_recv.at[2 + n], (to, me_tn))

        each(N - 1, one)
        pltpu.make_async_copy(src.at[n, me_dp], dst.at[n, me_dp], rs_recv.at[2 + n]).start()

    sum_z_out(0, lacc, lrecv)

    def store(c):
        at = pl.ds(pl.multiple_of(c * TC, TC), TC)
        return (
            pltpu.make_async_copy(outv.at[c], out_hbm.at[:, at], store_sem.at[0, c]),
            pltpu.make_async_copy(ginv.at[c], gin_hbm.at[:, at], store_sem.at[1, c]),
        )

    def stage_c_out(c):
        wait_bytes(s3r.at[c], a2a_recv.at[2, c])
        moved = s3r[c].reshape(512, TC)
        row_k = lax.rem(iota((512, 128), 0), 4)
        for p in range(2):
            part = mm_nt(moved, gv[c, pl.ds(256 * p, 256), :])
            part = jnp.where(row_k == 2 * p, part[:, :128], jnp.where(row_k == 2 * p + 1, part[:, 128:], 0.0))
            r2acc[...] += part.reshape(2, NZ, 2, 16, 128)

        @pl.when(c == NC - 1)
        def _():
            sum_z_out(1, r2acc, r2recv)

        outv[c] = mm(wcd[...], moved).astype(BF)
        store(c)[0].start()

    def stage_c_in(c):
        col_k = lax.rem(iota((128, 256), 1), 4)

        def half(q):
            wait_bytes(bor.at[c, q], a2a_recv.at[3 + q, c])
            moved = bor[c, q].reshape(256, TC)
            for p in range(2):
                part = mm_nt(xv[c, pl.ds(256 * p, 256), :], moved)
                part = jnp.where(col_k == 2 * p, part[:128], jnp.where(col_k == 2 * p + 1, part[128:], 0.0))
                r1acc[q] += part.reshape(N, 8, 256)

            @pl.when(c == NC - 1)
            def _():
                sum_out(q, r1acc, r1recv)

        each(2, half)
        ginv[c] = mm(wcu[...], bor[c].reshape(512, TC)).astype(BF)
        store(c)[1].start()

    def stage_c(c):
        @pl.when(c == NC - 1)
        def _():
            sum_z_in(0, lrecv, lsum, lpair)

        stage_c_out(c)
        stage_c_in(c)

    each(NC, stage_c)

    sum_z_in(1, r2recv, r2sum, r2pair)
    total = sum_pair(0, lsum, lpair)
    l1_ref[...] = total[:2].reshape(L_SHAPE)
    l2_ref[...] = total[2:].reshape(L_SHAPE)
    half_sums = []
    for q in range(2):
        wait_bytes(r1recv.at[q], rs_recv.at[2 + q])
        total = r1recv[q, 0]
        for d in range(1, N):
            total = total + r1recv[q, d]
        half_sums.append(total)
    total = jnp.concatenate(half_sums, axis=1)
    for k in range(4):
        r1_ref[k] = jnp.dot(total, spread(k).astype(F32), preferred_element_type=F32, precision=lax.Precision.HIGHEST)
    r2rows[...] = sum_pair(1, r2sum, r2pair).reshape(32, 128)
    for k in range(4):
        r2_ref[k] = r2rows[pl.ds(k, 8, stride=4), :]

    def finish(c):
        copy_out, copy_in = store(c)
        copy_out.wait()
        copy_in.wait()

    each(NC, finish)
    for n, (_, whole) in enumerate(first + second):
        wait_bytes(whole.at[:, pl.ds(0, N - 1)], ag_send.at[n])
    for n, src in enumerate((s1s, b3s, s3s, bos)):
        wait_bytes(src.at[:, :, pl.ds(0, N - 1)], a2a_send.at[n])
    wait_bytes(lrecv.at[pl.ds(0, NZ - 1)], rs_send.at[0])
    wait_bytes(r2recv.at[pl.ds(0, NZ - 1)], rs_send.at[1])
    for q in range(2):
        wait_bytes(r1recv.at[q, pl.ds(0, N - 1)], rs_send.at[2 + q])
    wait_bytes(lpair, half_send.at[0])
    wait_bytes(r2pair, half_send.at[1])


def local(activations, cotangent, first_up, second_up, second_down, first_down):
    any_spec = pl.BlockSpec(memory_space=pl.ANY)
    vmem = pl.BlockSpec(memory_space=pltpu.VMEM)
    scratch = [
        pltpu.VMEM((NC, 512, TC), BF),
        pltpu.VMEM((NC, 512, TC), BF),
        pltpu.VMEM((4, N, 8, 128), BF),
        pltpu.VMEM((4, N, 8, 128), BF),
        pltpu.VMEM((2, N) + B_SHAPE[1:], BF),
        pltpu.VMEM((2, N) + B_SHAPE[1:], BF),
        pltpu.VMEM((512, 512), BF),
        pltpu.VMEM((512, 512), BF),
        pltpu.VMEM((512, 512), BF),
        pltpu.VMEM((512, 512), BF),
        pltpu.VMEM((2, 4, 256, 256), BF),
        pltpu.VMEM((2, 4, 256, 256), BF),
        pltpu.VMEM((2, 256, 1024), BF),
        pltpu.VMEM((2, 256, 1024), BF),
        pltpu.VMEM((NC, 2, N, 16, TC), BF),
        pltpu.VMEM((NC, 2, N, 16, TC), BF),
        pltpu.VMEM((NC, 2, N, 16, TC), BF),
        pltpu.VMEM((NC, 2, N, 16, TC), BF),
        pltpu.VMEM((NC, 2, N, 16, TC), BF),
        pltpu.VMEM((NC, 2, N, 16, TC), BF),
        pltpu.VMEM((NC, 2, N, 16, TC), BF),
        pltpu.VMEM((NC, 2, N, 16, TC), BF),
        pltpu.VMEM((2, 1024, TC), BF),
        pltpu.VMEM((2, 1024, TC), F32),
        pltpu.VMEM((1024, TC), BF),
        pltpu.VMEM((NC, 512, TC), BF),
        pltpu.VMEM((NC, 512, TC), BF),
        pltpu.VMEM((4, NZ, 2, 16, 256), F32),
        pltpu.VMEM((2, N, 8, 256), F32),
        pltpu.VMEM((2, NZ, 2, 16, 128), F32),
        pltpu.VMEM((NZ, 4, 2, 16, 256), F32),
        pltpu.VMEM((2, N, 8, 256), F32),
        pltpu.VMEM((NZ, 2, 2, 16, 128), F32),
        pltpu.VMEM((2, 4, 16, 256), F32),
        pltpu.VMEM((2, 2, 16, 128), F32),
        pltpu.VMEM((4, 16, 256), F32),
        pltpu.VMEM((2, 16, 128), F32),
        pltpu.VMEM((32, 128), F32),
        pltpu.SemaphoreType.DMA((4,)),
        pltpu.SemaphoreType.DMA((4,)),
        pltpu.SemaphoreType.DMA((2,)),
        pltpu.SemaphoreType.DMA((4,)),
        pltpu.SemaphoreType.DMA((5, NC)),
        pltpu.SemaphoreType.DMA((4,)),
        pltpu.SemaphoreType.DMA((4,)),
        pltpu.SemaphoreType.DMA((2,)),
        pltpu.SemaphoreType.DMA((2,)),
        pltpu.SemaphoreType.DMA((2, NC)),
        pltpu.SemaphoreType.DMA((2, NC)),
    ]
    out, gin, r1, l1, l2, r2 = pl.pallas_call(
        kernel,
        name="monarch_layer",
        out_shape=(
            jax.ShapeDtypeStruct((512, 2048), BF),
            jax.ShapeDtypeStruct((512, 2048), BF),
            jax.ShapeDtypeStruct((4, 8, 128), F32),
            jax.ShapeDtypeStruct(L_SHAPE, F32),
            jax.ShapeDtypeStruct(L_SHAPE, F32),
            jax.ShapeDtypeStruct((4, 8, 128), F32),
        ),
        in_specs=[any_spec] * 6,
        out_specs=(any_spec, any_spec, vmem, vmem, vmem, vmem),
        scratch_shapes=scratch,
        compiler_params=pltpu.CompilerParams(
            collective_id=0, has_side_effects=True, vmem_limit_bytes=60 * 1024 * 1024
        ),
    )(
        activations, cotangent, first_up, first_down,
        second_up.reshape(B_SHAPE), second_down.reshape(B_SHAPE),
    )
    return out, gin, r1, l1.reshape(8, 4, 256), l2.reshape(8, 4, 256), r2


def solution(mesh):
    spec = (P("tensor", "dp"),) * 2 + (P("tensor", "dp", None),) * 4
    return jax.shard_map(local, mesh=mesh, in_specs=spec, out_specs=spec, check_vma=False)
```

time: 150 us -> 134 us (0.89)
  Pallas kernels: 138 us -> 126 us
  local copies, waits for them, and re-layouts: 11.3 us -> 7.09 us
    pallas_call x1, Pallas kernels: 138 us -> 126 us  [local(): pl.pallas_call(kernel, name='monarch_layer', out_shape=(jax.ShapeDtypeStr...]
    reshape x4 -> x0, local copies, waits for them, and re-layouts: 5.43 us -> none  [the longest x2 2.77 us: local(): return (out, gin, r1, l1.reshape(8, 4, 256), l2.reshape(8, 4, 256), r2)]
    unnamed x10 -> x16, local copies, waits for them, and re-layouts: 5.85 us -> 7.09 us
where the time goes in v2:
time: 134 us
  Pallas kernels  126 us (94%)
  local copies, waits for them, and re-layouts  7.09 us (5%)
    pallas_call x1, Pallas kernels, local(): pl.pallas_call(kernel, name='monarch_layer', out_shape=(jax.ShapeDtypeStr...  126 us
    unnamed x16, local copies, waits for them, and re-layouts  7.09 us

profile of v2, /device:TPU:1, one launch (start us, length us, event | category | flops | bytes accessed | tf_op | source)
XLA Modules:
  0.0 133.8 jit_solution(8268426280003613888)
XLA Ops:
  0.6 126.0 %monarch_layer.1 = (bf16[512,2048]{1,0:T(8,128)(2,1)}, bf16[512,2048]{1,0:T(8,128)(2,1)}, f32[4,8,128]{2,1,0:T(8,128)}, f32[8,4,256]{2,1,0:T(4,128)}, f32[8,4,256]{2,1,0:T(4,128)}, /*index=5*/f32[4,8,128]{2,1,0:T(8,128)}) custom-call(bf16[512,2048]{1,0:T(8,128)(2,1)} %x_hbm.1, bf16[512,2048]{1,0:T(8,128)(2,1)} %g_hbm.1, bf16[4,8,128]{2,1,0:T(8,128)(2,1)} %au_hbm.1, ...), custom_call_target="tpu_custom_call" | custom-call | tf_op jit(solution)/shard_map/monarch_layer/pallas_call | solution.py:401
  126.7 0.0 copy-start
  126.7 3.3 %copy.18 = bf16[512,2048]{1,0:T(8,128)(2,1)} copy(bf16[512,2048]{1,0:T(8,128)(2,1)} %get-tuple-element.12) | data formatting | bytes 4194304
  130.0 0.0 copy-done
  130.0 0.0 copy-start.4
  130.0 0.0 copy-start.2
  130.0 0.0 copy-start.1
  130.0 0.0 copy-start.3
  130.0 1.3 copy.19
  131.3 0.0 copy-done.4
  131.3 0.6 copy.20
  131.9 0.0 copy-done.2
  131.9 0.6 copy.21
  132.5 0.0 copy-done.1
  132.5 0.6 copy.22
  133.2 0.0 copy-done.3
  133.2 0.6 copy.23
Async XLA Ops:
  126.7 3.3 %copy-start = (bf16[512,2048]{1,0:T(8,128)(2,1)S(1)}, bf16[512,2048]{1,0:T(8,128)(2,1)}, u32[]{:S(2)}) copy-start(bf16[512,2048]{1,0:T(8,128)(2,1)} %get-tuple-element.13) | copy-start | bytes 6291460
  130.0 1.3 %copy-start.4 = (f32[4,8,128]{2,1,0:T(8,128)S(1)}, f32[4,8,128]{2,1,0:T(8,128)}, u32[]{:S(2)}) copy-start(f32[4,8,128]{2,1,0:T(8,128)} %get-tuple-element.14) | copy-start | bytes 49156
  130.0 1.9 %copy-start.2 = (f32[8,4,256]{2,1,0:T(4,128)S(1)}, f32[8,4,256]{2,1,0:T(4,128)}, u32[]{:S(2)}) copy-start(f32[8,4,256]{2,1,0:T(4,128)} %get-tuple-element.15) | copy-start | bytes 98308
  130.0 2.6 %copy-start.1 = (f32[8,4,256]{2,1,0:T(4,128)S(1)}, f32[8,4,256]{2,1,0:T(4,128)}, u32[]{:S(2)}) copy-start(f32[8,4,256]{2,1,0:T(4,128)} %get-tuple-element.16) | copy-start | bytes 98308
  130.0 3.2 %copy-start.3 = (f32[4,8,128]{2,1,0:T(8,128)S(1)}, f32[4,8,128]{2,1,0:T(8,128)}, u32[]{:S(2)}) copy-start(f32[4,8,128]{2,1,0:T(8,128)} %get-tuple-element.17) | copy-start | bytes 49156

commit v3 on v2

--- a/solution.py
+++ b/solution.py
@@ -38,9 +38,9 @@
     out_hbm, gin_hbm, r1_ref, l1_ref, l2_ref, r2_ref,
     xv, gv, au, ad, bu, bd, wau, wad, wcu, wcd, wbu, wbd, wtu, wtd,
     s1s, b3s, s1r, b3r, s3s, bos, s3r, bor, hid, slope, bp, outv, ginv,
-    lacc, r1acc, r2acc, lrecv, r1recv, r2recv, lsum, r2sum, lpair, r2pair, r2rows,
+    perm, lacc, r1acc, r2acc, lrecv, r1recv, r2recv, lsum, r2sum, lpair, r2pair, r2rows,
     ag_send, ag_recv, pair_recv, a2a_send, a2a_recv, rs_send, rs_recv, half_send, half_recv,
-    load_sem, store_sem,
+    own_sem, load_sem, store_sem,
 ):
     me_dp = lax.axis_index("dp")
     me_tn = lax.axis_index("tensor")
@@ -68,7 +68,21 @@
         copy_x.start()
         copy_g.start()
 
+    first = ((au_hbm, au), (ad_hbm, ad))
+    second = ((bu_hbm, bu), (bd_hbm, bd))
+    own = [
+        pltpu.make_async_copy(shard, whole.at[:, me_dp], own_sem.at[n])
+        for n, (shard, whole) in enumerate(first + second)
+    ]
+    for copy in own:
+        copy.start()
     each(NC, start_load)
+
+    row, col = iota((512, 512), 0), iota((512, 512), 1)
+    place = 128 * lax.rem(row, 4) + 8 * lax.rem(row // 16, N) + 4 * (row // 256) + lax.rem(row // 4, 4)
+    perm[...] = (place == col).astype(BF)
+    for copy in own:
+        copy.wait()
     pl.semaphore_wait(barrier, 2 * (N - 1))
 
     def remote(src, dst, send, recv, peer):
@@ -80,24 +94,23 @@
     def wait_bytes(ref, sem):
         pltpu.make_async_copy(ref, ref, sem).wait()
 
-    first = ((au_hbm, au), (ad_hbm, ad))
-    for n, (shard, whole) in enumerate(first):
-        def gather_send(r, n=n, shard=shard, whole=whole):
-            remote(shard, whole.at[:, me_dp], ag_send.at[n], ag_recv.at[n], (lax.rem(me_dp + r + 1, N), me_tn))
+    for n, (_, whole) in enumerate(first):
+        def gather_send(r, n=n, whole=whole):
+            mine = whole.at[:, me_dp]
+            remote(mine, mine, ag_send.at[n], ag_recv.at[n], (lax.rem(me_dp + r + 1, N), me_tn))
 
         each(N - 1, gather_send)
-        pltpu.make_async_copy(shard, whole.at[:, me_dp], ag_recv.at[n]).start()
-
-    second = ((bu_hbm, bu), (bd_hbm, bd))
-    for n, (shard, whole) in enumerate(second):
-        remote(shard, whole.at[:, me_dp], ag_send.at[2 + n], pair_recv.at[n], (pair, me_tn))
-
-        def along_z(r, n=n, shard=shard, whole=whole):
+
+    for n, (_, whole) in enumerate(second):
+        mine = whole.at[:, me_dp]
+        remote(mine, mine, ag_send.at[2 + n], pair_recv.at[n], (pair, me_tn))
+
+        def along_z(r, n=n, whole=whole):
+            mine = whole.at[:, me_dp]
             to = 2 * lax.rem(me_z + r + 1, NZ) + me_xl
-            remote(shard, whole.at[:, me_dp], ag_send.at[2 + n], ag_recv.at[2 + n], (to, me_tn))
+            remote(mine, mine, ag_send.at[2 + n], ag_recv.at[2 + n], (to, me_tn))
 
         each(NZ - 1, along_z)
-        pltpu.make_async_copy(shard, whole.at[:, me_dp], ag_recv.at[2 + n]).start()
 
     def pass_on():
         for n, (_, whole) in enumerate(second):
@@ -110,9 +123,7 @@
             each(NZ - 1, along_z)
 
     def spread(k):
-        row = iota((512, 128), 0)
-        j = 8 * lax.rem(row // 16, N) + 4 * (row // 256) + lax.rem(row // 4, 4)
-        return jnp.logical_and(lax.rem(row, 4) == k, iota((512, 128), 1) == j).astype(BF)
+        return perm[:, pl.ds(128 * k, 128)]
 
     def square(ref, k):
         return ref[k].astype(F32).reshape(128, 128).astype(BF)
@@ -143,11 +154,11 @@
         b3s[c] = mm(wad[...], gv[c]).astype(BF).reshape(2, N, 16, TC)
         exchange(c, 1, b3s, b3r)
 
-    wait_bytes(au, ag_recv.at[0])
+    wait_bytes(au.at[:, pl.ds(0, N - 1)], ag_recv.at[0])
     for k in range(4):
         wau[:, pl.ds(128 * k, 128)] = mm_nt(spread(k), square(au, k)).astype(BF)
     stage_a_up(0)
-    wait_bytes(ad, ag_recv.at[1])
+    wait_bytes(ad.at[:, pl.ds(0, N - 1)], ag_recv.at[1])
     for k in range(4):
         wad[:, pl.ds(128 * k, 128)] = mm(spread(k), square(ad, k)).astype(BF)
     stage_a_down(0)
@@ -164,7 +175,7 @@
         wcd[rows, :] = lax.dot_general(square(ad, k), spread(k), TN, preferred_element_type=F32).astype(BF)
 
     for n, (whole, wide, tall) in enumerate(((bu, wtu, wbu), (bd, wtd, wbd))):
-        wait_bytes(whole.at[:, pl.ds(0, N - 1)], ag_recv.at[2 + n])
+        wait_bytes(whole.at[:, pl.ds(0, N - 2)], ag_recv.at[2 + n])
         for q in range(2):
             block = whole[q].reshape(256, 256)
             flipped = block.astype(F32).T.astype(BF)
@@ -312,16 +323,6 @@
     total = sum_pair(0, lsum, lpair)
     l1_ref[...] = total[:2].reshape(L_SHAPE)
     l2_ref[...] = total[2:].reshape(L_SHAPE)
-    half_sums = []
-    for q in range(2):
-        wait_bytes(r1recv.at[q], rs_recv.at[2 + q])
-        total = r1recv[q, 0]
-        for d in range(1, N):
-            total = total + r1recv[q, d]
-        half_sums.append(total)
-    total = jnp.concatenate(half_sums, axis=1)
-    for k in range(4):
-        r1_ref[k] = jnp.dot(total, spread(k).astype(F32), preferred_element_type=F32, precision=lax.Precision.HIGHEST)
     r2rows[...] = sum_pair(1, r2sum, r2pair).reshape(32, 128)
     for k in range(4):
         r2_ref[k] = r2rows[pl.ds(k, 8, stride=4), :]
@@ -338,15 +339,38 @@
         wait_bytes(src.at[:, :, pl.ds(0, N - 1)], a2a_send.at[n])
     wait_bytes(lrecv.at[pl.ds(0, NZ - 1)], rs_send.at[0])
     wait_bytes(r2recv.at[pl.ds(0, NZ - 1)], rs_send.at[1])
+    wait_bytes(lpair, half_send.at[0])
+    wait_bytes(r2pair, half_send.at[1])
+
+    ordered = jnp.zeros((8, 512), F32)
+    for q in range(2):
+        wait_bytes(r1recv.at[q], rs_recv.at[2 + q])
+        total = r1recv[q, 0]
+        for d in range(1, N):
+            total = total + r1recv[q, d]
+        high = total.astype(BF).astype(F32)
+        middle = (total - high).astype(BF).astype(F32)
+        parts = jnp.concatenate((high, middle, total - high - middle), axis=0).astype(BF)
+        moved = mm(parts, perm[pl.ds(256 * q, 256), :])
+        ordered = ordered + (moved[:8] + moved[8:16] + moved[16:])
+    for k in range(4):
+        r1_ref[k] = ordered[:, 128 * k : 128 * k + 128]
     for q in range(2):
         wait_bytes(r1recv.at[q, pl.ds(0, N - 1)], rs_send.at[2 + q])
-    wait_bytes(lpair, half_send.at[0])
-    wait_bytes(r2pair, half_send.at[1])
+
+
+def settle(*refs):
+    copies = [pltpu.make_async_copy(refs[n], refs[6 + n], refs[12].at[n]) for n in range(6)]
+    for copy in copies:
+        copy.start()
+    for copy in copies:
+        copy.wait()
 
 
 def local(activations, cotangent, first_up, second_up, second_down, first_down):
     any_spec = pl.BlockSpec(memory_space=pl.ANY)
     vmem = pl.BlockSpec(memory_space=pltpu.VMEM)
+    hbm = pl.BlockSpec(memory_space=pltpu.HBM)
     scratch = [
         pltpu.VMEM((NC, 512, TC), BF),
         pltpu.VMEM((NC, 512, TC), BF),
@@ -375,6 +399,7 @@
         pltpu.VMEM((1024, TC), BF),
         pltpu.VMEM((NC, 512, TC), BF),
         pltpu.VMEM((NC, 512, TC), BF),
+        pltpu.VMEM((512, 512), BF),
         pltpu.VMEM((4, NZ, 2, 16, 256), F32),
         pltpu.VMEM((2, N, 8, 256), F32),
         pltpu.VMEM((2, NZ, 2, 16, 128), F32),
@@ -395,10 +420,11 @@
         pltpu.SemaphoreType.DMA((4,)),
         pltpu.SemaphoreType.DMA((2,)),
         pltpu.SemaphoreType.DMA((2,)),
+        pltpu.SemaphoreType.DMA((4,)),
         pltpu.SemaphoreType.DMA((2, NC)),
         pltpu.SemaphoreType.DMA((2, NC)),
     ]
-    out, gin, r1, l1, l2, r2 = pl.pallas_call(
+    results = pl.pallas_call(
         kernel,
         name="monarch_layer",
         out_shape=(
@@ -409,17 +435,32 @@
             jax.ShapeDtypeStruct(L_SHAPE, F32),
             jax.ShapeDtypeStruct((4, 8, 128), F32),
         ),
-        in_specs=[any_spec] * 6,
+        in_specs=[hbm] * 6,
         out_specs=(any_spec, any_spec, vmem, vmem, vmem, vmem),
         scratch_shapes=scratch,
         compiler_params=pltpu.CompilerParams(
-            collective_id=0, has_side_effects=True, vmem_limit_bytes=60 * 1024 * 1024
+            collective_id=0, has_side_effects=True, vmem_limit_bytes=49 * 1024 * 1024
         ),
     )(
-        activations, cotangent, first_up, first_down,
-        second_up.reshape(B_SHAPE), second_down.reshape(B_SHAPE),
+        *(
+            pltpu.with_memory_space_constraint(value, pltpu.HBM)
+            for value in (
+                activations, cotangent, first_up, first_down,
+                second_up.reshape(B_SHAPE), second_down.reshape(B_SHAPE),
+            )
+        )
     )
-    return out, gin, r1, l1.reshape(8, 4, 256), l2.reshape(8, 4, 256), r2
+    return tuple(
+        pl.pallas_call(
+            settle,
+            name="settle",
+            out_shape=tuple(jax.ShapeDtypeStruct(r.shape, r.dtype) for r in results),
+            in_specs=[any_spec] * 6,
+            out_specs=(hbm,) * 6,
+            compiler_params=pltpu.CompilerParams(vmem_limit_bytes=1024 * 1024),
+            scratch_shapes=[pltpu.SemaphoreType.DMA((6,))],
+        )(*results)
+    )
 
 
 def solution(mesh):

time: 134 us -> 127 us (0.948)
  local copies, waits for them, and re-layouts: 7.09 us -> 0 us
    unnamed x16 -> x0, local copies, waits for them, and re-layouts: 7.09 us -> none
    pallas_call x1, Pallas kernels: 126 us -> 124 us  [local(): pl.pallas_call(kernel, name='monarch_layer', out_shape=(jax.ShapeDtypeStr...]
    pallas_call x0 -> x1, Pallas kernels: none -> 2.07 us  [local(): pl.pallas_call(settle, name='settle', out_shape=tuple((jax.ShapeDtypeStru...]
where the time goes in v3:
time: 127 us
  Pallas kernels  126 us (99%)
    pallas_call x1, Pallas kernels, local(): pl.pallas_call(kernel, name='monarch_layer', out_shape=(jax.ShapeDtypeStr...  124 us

profile of v3, /device:TPU:1, one launch (start us, length us, event | category | flops | bytes accessed | tf_op | source)
XLA Modules:
  0.0 126.6 jit_solution(10773537291578781147)
XLA Ops:
  0.6 123.9 %monarch_layer.1 = (bf16[512,2048]{1,0:T(8,128)(2,1)S(1)}, bf16[512,2048]{1,0:T(8,128)(2,1)S(1)}, f32[4,8,128]{2,1,0:T(8,128)S(1)}, f32[8,4,256]{2,1,0:T(4,128)S...) custom-call(bf16[512,2048]{1,0:T(8,128)(2,1)} %x_hbm.1, bf16[512,2048]{1,0:T(8,128)(2,1)} %g_hbm.1, ...), custom_call_target="tpu_custom_call" | custom-call | tf_op jit(solution)/shard_map/monarch_layer/pallas_call | solution.py:427
  124.5 2.1 %settle.1 = (bf16[512,2048]{1,0:T(8,128)(2,1)}, bf16[512,2048]{1,0:T(8,128)(2,1)}, f32[4,8,128]{2,1,0:T(8,128)}, f32[8,4,256]{2,1,0:T(4,128)}, f32[8,4,256]{2,1,0:T(4,128)}, /*index=5*/f32[4,8,128]{2,1,0:T(8,128)}) custom-call(bf16[512,2048]{1,0:T(8,128)(2,1)S(1)} %get-tuple-element.12.refs_0_, bf16[512,2048]{1,0:T(8,128)(2,1)S(1)} %get-tuple-element.13.refs_1_, ...), custom_call_target="tpu_custom_call" | custom-call | tf_op jit(solution)/shard_map/settle/pallas_call | solution.py:454

commit v4 on v3

--- a/solution.py
+++ b/solution.py
@@ -38,12 +38,21 @@
     out_hbm, gin_hbm, r1_ref, l1_ref, l2_ref, r2_ref,
     xv, gv, au, ad, bu, bd, wau, wad, wcu, wcd, wbu, wbd, wtu, wtd,
     s1s, b3s, s1r, b3r, s3s, bos, s3r, bor, hid, slope, bp, outv, ginv,
-    perm, lacc, r1acc, r2acc, lrecv, r1recv, r2recv, lsum, r2sum, lpair, r2pair, r2rows,
+    perm, lacc, r1acc, r2acc, r1out, r2out, lrecv, r1recv, r2recv, lsum, r2sum, lpair, r2pair, r2rows,
     ag_send, ag_recv, pair_recv, a2a_send, a2a_recv, rs_send, rs_recv, half_send, half_recv,
     own_sem, load_sem, store_sem,
 ):
     me_dp = lax.axis_index("dp")
     me_tn = lax.axis_index("tensor")
+    def far_first(i, size):
+        return size // 2 + ((i + 1) // 2) * (2 * lax.rem(i, 2) - 1)
+
+    def other_dp(i):
+        return lax.rem(me_dp + far_first(i, N), N)
+
+    def other_z(i):
+        return lax.rem(me_z + far_first(i, NZ), NZ)
+
     me_z = me_dp // 2
     me_xl = lax.rem(me_dp, 2)
     pair = 2 * me_z + 1 - me_xl
@@ -97,7 +106,7 @@
     for n, (_, whole) in enumerate(first):
         def gather_send(r, n=n, whole=whole):
             mine = whole.at[:, me_dp]
-            remote(mine, mine, ag_send.at[n], ag_recv.at[n], (lax.rem(me_dp + r + 1, N), me_tn))
+            remote(mine, mine, ag_send.at[n], ag_recv.at[n], (other_dp(r), me_tn))
 
         each(N - 1, gather_send)
 
@@ -107,7 +116,7 @@
 
         def along_z(r, n=n, whole=whole):
             mine = whole.at[:, me_dp]
-            to = 2 * lax.rem(me_z + r + 1, NZ) + me_xl
+            to = 2 * other_z(r) + me_xl
             remote(mine, mine, ag_send.at[2 + n], ag_recv.at[2 + n], (to, me_tn))
 
         each(NZ - 1, along_z)
@@ -117,7 +126,7 @@
             wait_bytes(whole.at[:, pair], pair_recv.at[n])
 
             def along_z(r, n=n, whole=whole):
-                to = 2 * lax.rem(me_z + r + 1, NZ) + me_xl
+                to = 2 * other_z(r) + me_xl
                 remote(whole.at[:, pair], whole.at[:, pair], ag_send.at[2 + n], ag_recv.at[2 + n], (to, me_tn))
 
             each(NZ - 1, along_z)
@@ -238,19 +247,21 @@
 
     def sum_z_out(n, acc, recv):
         def one(r):
-            to = lax.rem(me_z + r + 1, NZ)
+            to = other_z(r)
             remote(acc.at[:, to], recv.at[me_z], rs_send.at[n], rs_recv.at[n], (2 * to + me_xl, me_tn))
 
         each(NZ - 1, one)
         pltpu.make_async_copy(acc.at[:, me_z], recv.at[me_z], rs_recv.at[n]).start()
 
-    def sum_z_in(n, recv, sums, pair_ref):
+    def sum_z_in(n, recv, sums):
         wait_bytes(recv, rs_recv.at[n])
         for h in range(2):
-            total = recv[0, :, h]
+            total = recv[0, :, h].astype(F32)
             for d in range(1, NZ):
-                total = total + recv[d, :, h]
+                total = total + recv[d, :, h].astype(F32)
             sums[h] = total
+
+    def pair_out(n, sums, pair_ref):
         remote(sums.at[1 - me_xl], pair_ref, half_send.at[n], half_recv.at[n], (pair, me_tn))
 
     def sum_pair(n, sums, pair_ref):
@@ -259,7 +270,7 @@
 
     def sum_out(n, src, dst):
         def one(r):
-            to = lax.rem(me_dp + r + 1, N)
+            to = other_dp(r)
             remote(src.at[n, to], dst.at[n, me_dp], rs_send.at[2 + n], rs_recv.at[2 + n], (to, me_tn))
 
         each(N - 1, one)
@@ -285,7 +296,8 @@
 
         @pl.when(c == NC - 1)
         def _():
-            sum_z_out(1, r2acc, r2recv)
+            r2out[...] = r2acc[...].astype(BF)
+            sum_z_out(1, r2out, r2recv)
 
         outv[c] = mm(wcd[...], moved).astype(BF)
         store(c)[0].start()
@@ -303,23 +315,30 @@
 
             @pl.when(c == NC - 1)
             def _():
-                sum_out(q, r1acc, r1recv)
+                r1out[q] = r1acc[q].astype(BF)
+                sum_out(q, r1out, r1recv)
 
         each(2, half)
+
+        @pl.when(c == NC - 1)
+        def _():
+            pair_out(0, lsum, lpair)
+
         ginv[c] = mm(wcu[...], bor[c].reshape(512, TC)).astype(BF)
         store(c)[1].start()
 
     def stage_c(c):
         @pl.when(c == NC - 1)
         def _():
-            sum_z_in(0, lrecv, lsum, lpair)
+            sum_z_in(0, lrecv, lsum)
 
         stage_c_out(c)
         stage_c_in(c)
 
     each(NC, stage_c)
 
-    sum_z_in(1, r2recv, r2sum, r2pair)
+    sum_z_in(1, r2recv, r2sum)
+    pair_out(1, r2sum, r2pair)
     total = sum_pair(0, lsum, lpair)
     l1_ref[...] = total[:2].reshape(L_SHAPE)
     l2_ref[...] = total[2:].reshape(L_SHAPE)
@@ -345,9 +364,9 @@
     ordered = jnp.zeros((8, 512), F32)
     for q in range(2):
         wait_bytes(r1recv.at[q], rs_recv.at[2 + q])
-        total = r1recv[q, 0]
+        total = r1recv[q, 0].astype(F32)
         for d in range(1, N):
-            total = total + r1recv[q, d]
+            total = total + r1recv[q, d].astype(F32)
         high = total.astype(BF).astype(F32)
         middle = (total - high).astype(BF).astype(F32)
         parts = jnp.concatenate((high, middle, total - high - middle), axis=0).astype(BF)
@@ -403,9 +422,11 @@
         pltpu.VMEM((4, NZ, 2, 16, 256), F32),
         pltpu.VMEM((2, N, 8, 256), F32),
         pltpu.VMEM((2, NZ, 2, 16, 128), F32),
+        pltpu.VMEM((2, N, 8, 256), BF),
+        pltpu.VMEM((2, NZ, 2, 16, 128), BF),
         pltpu.VMEM((NZ, 4, 2, 16, 256), F32),
-        pltpu.VMEM((2, N, 8, 256), F32),
-        pltpu.VMEM((NZ, 2, 2, 16, 128), F32),
+        pltpu.VMEM((2, N, 8, 256), BF),
+        pltpu.VMEM((NZ, 2, 2, 16, 128), BF),
         pltpu.VMEM((2, 4, 16, 256), F32),
         pltpu.VMEM((2, 2, 16, 128), F32),
         pltpu.VMEM((4, 16, 256), F32),

time: 127 us -> 121 us (0.953)
  Pallas kernels: 126 us -> 120 us
    pallas_call x1, Pallas kernels: 124 us -> 118 us  [local(): pl.pallas_call(kernel, name='monarch_layer', out_shape=(jax.ShapeDtypeStr...]
where the time goes in v4:
time: 121 us
  Pallas kernels  120 us (99%)
    pallas_call x1, Pallas kernels, local(): pl.pallas_call(kernel, name='monarch_layer', out_shape=(jax.ShapeDtypeStr...  118 us

profile of v4, /device:TPU:1, one launch (start us, length us, event | category | flops | bytes accessed | tf_op | source)
XLA Modules:
  0.0 120.7 jit_solution(16729440919119945965)
XLA Ops:
  0.6 118.0 %monarch_layer.1 = (bf16[512,2048]{1,0:T(8,128)(2,1)S(1)}, bf16[512,2048]{1,0:T(8,128)(2,1)S(1)}, f32[4,8,128]{2,1,0:T(8,128)S(1)}, f32[8,4,256]{2,1,0:T(4,128)S...) custom-call(bf16[512,2048]{1,0:T(8,128)(2,1)} %x_hbm.1, bf16[512,2048]{1,0:T(8,128)(2,1)} %g_hbm.1, ...), custom_call_target="tpu_custom_call" | custom-call | tf_op jit(solution)/shard_map/monarch_layer/pallas_call | solution.py:448
  118.6 2.1 %settle.1 = (bf16[512,2048]{1,0:T(8,128)(2,1)}, bf16[512,2048]{1,0:T(8,128)(2,1)}, f32[4,8,128]{2,1,0:T(8,128)}, f32[8,4,256]{2,1,0:T(4,128)}, f32[8,4,256]{2,1,0:T(4,128)}, /*index=5*/f32[4,8,128]{2,1,0:T(8,128)}) custom-call(bf16[512,2048]{1,0:T(8,128)(2,1)S(1)} %get-tuple-element.12.refs_0_, bf16[512,2048]{1,0:T(8,128)(2,1)S(1)} %get-tuple-element.13.refs_1_, ...), custom_call_target="tpu_custom_call" | custom-call | tf_op jit(solution)/shard_map/settle/pallas_call | solution.py:475

commit v5 on v4

--- a/solution.py
+++ b/solution.py
@@ -11,6 +11,7 @@
 NZ = 8
 NC = 4
 TC = 512
+PIECES = 4
 B_SHAPE = (2, 4, 4, 256)
 L_SHAPE = (8, 4, 256)
 NT = (((1,), (1,)), ((), ()))
@@ -37,8 +38,8 @@
     x_hbm, g_hbm, au_hbm, ad_hbm, bu_hbm, bd_hbm,
     out_hbm, gin_hbm, r1_ref, l1_ref, l2_ref, r2_ref,
     xv, gv, au, ad, bu, bd, wau, wad, wcu, wcd, wbu, wbd, wtu, wtd,
-    s1s, b3s, s1r, b3r, s3s, bos, s3r, bor, hid, slope, bp, outv, ginv,
-    perm, lacc, r1acc, r2acc, r1out, r2out, lrecv, r1recv, r2recv, lsum, r2sum, lpair, r2pair, r2rows,
+    s1s, b3s, s1r, b3r, s3s, bos, s3r, bor, hid, slope, bp,
+    perm, lacc, r1acc, r2acc, r1out, lrecv, r1recv, r2recv, lsum, r2sum, lpair, r2pair, r2rows,
     ag_send, ag_recv, pair_recv, a2a_send, a2a_recv, rs_send, rs_recv, half_send, half_recv,
     own_sem, load_sem, store_sem,
 ):
@@ -199,7 +200,8 @@
     r1acc[...] = jnp.zeros_like(r1acc)
     r2acc[...] = jnp.zeros_like(r2acc)
 
-    def stage_b(c):
+    def stage_b_forward(c):
+        slot = lax.rem(c, 2)
         wait_bytes(s1r.at[c], a2a_recv.at[0, c])
 
         def forward(q):
@@ -209,14 +211,17 @@
                 pre = mm(wbu[q, b], moved)
                 half = 0.5 * (1.0 + lax.erf(pre * 0.7071067811865476))
                 rows = pl.ds(pl.multiple_of(256 * b, 256), 256)
-                hid[q, rows, :] = (pre * half).astype(BF)
-                slope[q, rows, :] = half + pre * jnp.exp(-0.5 * pre * pre) * 0.3989422804014327
+                hid[slot, q, rows, :] = (pre * half).astype(BF)
+                slope[slot, q, rows, :] = half + pre * jnp.exp(-0.5 * pre * pre) * 0.3989422804014327
 
             each(4, block)
-            s3s[c, q] = mm(wtd[q], hid[q]).astype(BF).reshape(N, 16, TC)
+            s3s[c, q] = mm(wtd[q], hid[slot, q]).astype(BF).reshape(N, 16, TC)
 
         each(2, forward)
         exchange(c, 2, s3s, s3r)
+
+    def stage_b_backward(c):
+        slot = lax.rem(c, 2)
         wait_bytes(b3r.at[c], a2a_recv.at[1, c])
 
         def backward(q):
@@ -226,7 +231,7 @@
 
             def slopes(b):
                 rows = pl.ds(pl.multiple_of(256 * b, 256), 256)
-                bp[rows, :] = (mm(wbd[q, b], back) * slope[q, rows, :]).astype(BF)
+                bp[rows, :] = (mm(wbd[q, b], back) * slope[slot, q, rows, :]).astype(BF)
 
             each(4, slopes)
             bos[c, q] = mm(wtu[q], bp[...]).astype(BF).reshape(N, 16, TC)
@@ -235,7 +240,7 @@
             def sums(b):
                 rows = pl.ds(pl.multiple_of(256 * b, 256), 256)
                 part_one = jnp.where(row_j == b, mm_nt(moved, bp[rows, :]), 0.0)
-                part_two = jnp.where(row_j == b, mm_nt(back, hid[q, rows, :]), 0.0)
+                part_two = jnp.where(row_j == b, mm_nt(back, hid[slot, q, rows, :]), 0.0)
                 lacc[q] += part_one.reshape(NZ, 2, 16, 256)
                 lacc[2 + q] += part_two.reshape(NZ, 2, 16, 256)
 
@@ -243,7 +248,20 @@
 
         each(2, backward)
 
-    each(NC, stage_b)
+    def stage_b(step):
+        @pl.when(step < NC)
+        def _():
+            stage_b_forward(step)
+
+        @pl.when(step < NC - 2)
+        def _():
+            stage_b_backward(step)
+
+        @pl.when(step >= NC - 1)
+        def _():
+            stage_b_backward(step - 1)
+
+    each(NC + 1, stage_b)
 
     def sum_z_out(n, acc, recv):
         def one(r):
@@ -281,8 +299,8 @@
     def store(c):
         at = pl.ds(pl.multiple_of(c * TC, TC), TC)
         return (
-            pltpu.make_async_copy(outv.at[c], out_hbm.at[:, at], store_sem.at[0, c]),
-            pltpu.make_async_copy(ginv.at[c], gin_hbm.at[:, at], store_sem.at[1, c]),
+            pltpu.make_async_copy(s3r.at[c], out_hbm.at[:, :, :, at], store_sem.at[0, c]),
+            pltpu.make_async_copy(bor.at[c], gin_hbm.at[:, :, :, at], store_sem.at[1, c]),
         )
 
     def stage_c_out(c):
@@ -296,10 +314,9 @@
 
         @pl.when(c == NC - 1)
         def _():
-            r2out[...] = r2acc[...].astype(BF)
-            sum_z_out(1, r2out, r2recv)
-
-        outv[c] = mm(wcd[...], moved).astype(BF)
+            sum_z_out(1, r2acc, r2recv)
+
+        s3r[c] = mm(wcd[...], moved).astype(BF).reshape(2, N, 16, TC)
         store(c)[0].start()
 
     def stage_c_in(c):
@@ -323,22 +340,31 @@
         @pl.when(c == NC - 1)
         def _():
             pair_out(0, lsum, lpair)
-
-        ginv[c] = mm(wcu[...], bor[c].reshape(512, TC)).astype(BF)
+            sum_z_in(1, r2recv, r2sum)
+            pair_out(1, r2sum, r2pair)
+
+        bor[c] = mm(wcu[...], bor[c].reshape(512, TC)).astype(BF).reshape(2, N, 16, TC)
         store(c)[1].start()
 
-    def stage_c(c):
-        @pl.when(c == NC - 1)
+    def stage_c(step):
+        @pl.when(step < NC)
+        def _():
+            stage_c_out(step)
+
+        @pl.when(step < NC - 2)
+        def _():
+            stage_c_in(step)
+
+        @pl.when(step == NC)
         def _():
             sum_z_in(0, lrecv, lsum)
 
-        stage_c_out(c)
-        stage_c_in(c)
-
-    each(NC, stage_c)
-
-    sum_z_in(1, r2recv, r2sum)
-    pair_out(1, r2sum, r2pair)
+        @pl.when(step >= NC - 1)
+        def _():
+            stage_c_in(step - 1)
+
+    each(NC + 1, stage_c)
+
     total = sum_pair(0, lsum, lpair)
     l1_ref[...] = total[:2].reshape(L_SHAPE)
     l2_ref[...] = total[2:].reshape(L_SHAPE)
@@ -379,7 +405,14 @@
 
 
 def settle(*refs):
-    copies = [pltpu.make_async_copy(refs[n], refs[6 + n], refs[12].at[n]) for n in range(6)]
+    sems = refs[12]
+    copies = []
+    for n in range(6):
+        pieces = PIECES if n < 2 else 1
+        size = refs[n].shape[0] // pieces
+        for p in range(pieces):
+            rows = pl.ds(p * size, size)
+            copies.append(pltpu.make_async_copy(refs[n].at[rows], refs[6 + n].at[rows], sems.at[n, p]))
     for copy in copies:
         copy.start()
     for copy in copies:
@@ -413,20 +446,17 @@
         pltpu.VMEM((NC, 2, N, 16, TC), BF),
         pltpu.VMEM((NC, 2, N, 16, TC), BF),
         pltpu.VMEM((NC, 2, N, 16, TC), BF),
-        pltpu.VMEM((2, 1024, TC), BF),
-        pltpu.VMEM((2, 1024, TC), F32),
+        pltpu.VMEM((2, 2, 1024, TC), BF),
+        pltpu.VMEM((2, 2, 1024, TC), F32),
         pltpu.VMEM((1024, TC), BF),
-        pltpu.VMEM((NC, 512, TC), BF),
-        pltpu.VMEM((NC, 512, TC), BF),
         pltpu.VMEM((512, 512), BF),
         pltpu.VMEM((4, NZ, 2, 16, 256), F32),
         pltpu.VMEM((2, N, 8, 256), F32),
         pltpu.VMEM((2, NZ, 2, 16, 128), F32),
         pltpu.VMEM((2, N, 8, 256), BF),
-        pltpu.VMEM((2, NZ, 2, 16, 128), BF),
         pltpu.VMEM((NZ, 4, 2, 16, 256), F32),
         pltpu.VMEM((2, N, 8, 256), BF),
-        pltpu.VMEM((NZ, 2, 2, 16, 128), BF),
+        pltpu.VMEM((NZ, 2, 2, 16, 128), F32),
         pltpu.VMEM((2, 4, 16, 256), F32),
         pltpu.VMEM((2, 2, 16, 128), F32),
         pltpu.VMEM((4, 16, 256), F32),
@@ -449,8 +479,8 @@
         kernel,
         name="monarch_layer",
         out_shape=(
-            jax.ShapeDtypeStruct((512, 2048), BF),
-            jax.ShapeDtypeStruct((512, 2048), BF),
+            jax.ShapeDtypeStruct((2, N, 16, 2048), BF),
+            jax.ShapeDtypeStruct((2, N, 16, 2048), BF),
             jax.ShapeDtypeStruct((4, 8, 128), F32),
             jax.ShapeDtypeStruct(L_SHAPE, F32),
             jax.ShapeDtypeStruct(L_SHAPE, F32),
@@ -471,6 +501,7 @@
             )
         )
     )
+    results = tuple(r.reshape(512, 2048) for r in results[:2]) + tuple(results[2:])
     return tuple(
         pl.pallas_call(
             settle,
@@ -479,7 +510,7 @@
             in_specs=[any_spec] * 6,
             out_specs=(hbm,) * 6,
             compiler_params=pltpu.CompilerParams(vmem_limit_bytes=1024 * 1024),
-            scratch_shapes=[pltpu.SemaphoreType.DMA((6,))],
+            scratch_shapes=[pltpu.SemaphoreType.DMA((6, PIECES))],
         )(*results)
     )
 

time: 121 us -> 121 us (level)
  no operation moved by 1% of the time
where the time goes in v5:
time: 121 us
  Pallas kernels  120 us (99%)
    pallas_call x1, Pallas kernels, local(): pl.pallas_call(kernel, name='monarch_layer', out_shape=(jax.ShapeDtypeStr...  118 us

profile of v5, /device:TPU:1, one launch (start us, length us, event | category | flops | bytes accessed | tf_op | source)
XLA Modules:
  0.0 120.8 jit_solution(2945152632714586587)
XLA Ops:
  0.6 117.9 %monarch_layer.1 = (bf16[2,16,16,2048]{3,2,1,0:T(8,128)(2,1)S(1)}, bf16[2,16,16,2048]{3,2,1,0:T(8,128)(2,1)S(1)}, f32[4,8,128]{2,1,0:T(8,128)S(1)}, f32[8,4,256]...) custom-call(bf16[512,2048]{1,0:T(8,128)(2,1)} %x_hbm.1, bf16[512,2048]{1,0:T(8,128)(2,1)} %g_hbm.1, ...), custom_call_target="tpu_custom_call" | custom-call | tf_op jit(solution)/shard_map/monarch_layer/pallas_call | solution.py:478
  118.5 2.2 %settle.1 = (bf16[512,2048]{1,0:T(8,128)(2,1)}, bf16[512,2048]{1,0:T(8,128)(2,1)}, f32[4,8,128]{2,1,0:T(8,128)}, f32[8,4,256]{2,1,0:T(4,128)}, f32[8,4,256]{2,1,0:T(4,128)}, /*index=5*/f32[4,8,128]{2,1,0:T(8,128)}) custom-call(bf16[512,2048]{1,0:T(8,128)(2,1)S(1)} %bitcast.4, bf16[512,2048]{1,0:T(8,128)(2,1)S(1)} %bitcast.5, ...), custom_call_target="tpu_custom_call" | custom-call | tf_op jit(solution)/shard_map/settle/pallas_call | solution.py:506
